TPU v7x, 256 devices: a whole 4x4x8 slice. The times are simulated.
256 devices in a mesh: dp: 8 (over z_lo, core), mp: 16 (over x, y), group: 2 (over z_hi).
Axes of the slice: x: 4, y: 4, z: 8 (z_hi: 2, z_lo: 4; z = z_hi * 4 + z_lo), core: 2. Of those that a mesh axis runs over, the one named last changes fastest.
Arguments:
- hidden: bfloat16 [1024, 8192], P('dp', 'mp'), may hold values from -6 to 6
- neighbour_ids: int32 [16, 2, 128], P('dp', 'group'), may hold values from 0 to 65535, as said below
- counts: int32 [16], P('dp'), may hold values from 0 to 2
- embed_table: bfloat16 [65536, 8192], P(('dp', 'group'), 'mp'), may hold values from -6 to 6
- w_query: bfloat16 [8192, 4096], P('group', 'mp'), may hold values from -0.0625 to 0.0625
- w_key: bfloat16 [8192, 4096], P('group', 'mp'), may hold values from -0.0625 to 0.0625
- w_value: bfloat16 [8192, 4096], P('group', 'mp'), may hold values from -0.0625 to 0.0625
- w_out: bfloat16 [4096, 8192], P('mp', 'group'), may hold values from -0.09375 to 0.09375
- grad_out: bfloat16 [1024, 8192], P('dp', 'mp'), may hold values from -6 to 6
Outputs:
- output: float32 [1024, 8192], P('dp', 'mp')
- grad_hidden: float32 [1024, 8192], P('dp', 'mp')
- grad_neighbours: float32 [16, 2, 128, 8192], P('dp', 'group', None, 'mp')
Inputs may be any that keep to these rules, and one draw needn't show every extreme that they name: `neighbour_ids`: token ids of the retrieved neighbours; the ids are split into 16 owners of 4096 consecutive ids each; of the 256 ids of one window's neighbour k (blocks of one window, one k), at most 64 belong to one owner, and exactly 64 belong to some owner. neighbours k < counts[c] of block c are used, the others are masked.
All inputs are finite; a program needn't handle non-finite values.
Results may differ from a plain program's by a relative error of at most 0.019.
Values may be sent and summed in bfloat16 or wider, within the bound.
A program may use at most 128 MiB of HBM per device.

v0:
```python
import math
import jax
import jax.numpy as jnp
from jax import lax
from jax.sharding import PartitionSpec as P

HD = 128
BLOCK = 64
RET = 128


def contract(left, right):
    return lax.dot_general(
        left, right, (((1,), (1,)), ((), ())), preferred_element_type=jnp.float32
    )


def per_device(
    hidden, neighbour_ids, counts, embed_table, w_query, w_key, w_value, w_out, grad_out
):
    tail_rows = BLOCK - 1
    rows_here = hidden.shape[0]
    blocks_here = rows_here // BLOCK
    heads_here = w_query.shape[1] // HD
    inv_root = 1.0 / math.sqrt(HD)
    keep_rows = rows_here - tail_rows
    pad_rows = jnp.zeros((tail_rows, hidden.shape[1]), jnp.bfloat16)
    query_rows = jnp.concatenate([hidden[tail_rows:], pad_rows], 0)
    grad_rows = jnp.concatenate([grad_out[tail_rows:], pad_rows], 0)
    full_query, full_grad = (
        lax.all_gather(query_rows, "mp", axis=1, tiled=True),
        lax.all_gather(grad_rows, "mp", axis=1, tiled=True),
    )
    flat_ids = neighbour_ids.reshape(-1)
    block_rows = embed_table.shape[0]
    owners = lax.axis_size("dp") * lax.axis_size("group")
    cap = flat_ids.shape[0] // 4
    every_id = (
        lax.all_gather(flat_ids.astype(jnp.float32), ("dp", "group"), axis=0, tiled=True)
        .astype(jnp.int32)
        .reshape(owners, -1)
    )
    owner = lax.axis_index("dp") * lax.axis_size("group") + lax.axis_index("group")
    local_ids = every_id - owner * block_rows
    inside = (local_ids >= 0) & (local_ids < block_rows)
    rank = jnp.cumsum(inside.astype(jnp.int32), axis=1) - 1
    slot_hit = inside[:, :, None] & (rank[:, :, None] == jnp.arange(cap)[None, None, :])
    send_rows = jnp.sum(jnp.where(slot_hit, local_ids[:, :, None], 0), axis=1)
    send_buf = embed_table[send_rows.reshape(-1)].reshape(owners, cap, -1)
    recv_buf = lax.all_to_all(send_buf, ("dp", "group"), 0, 0, tiled=True)
    own_owner = flat_ids // block_rows
    same_owner = own_owner[:, None] == jnp.arange(owners)[None, :]
    own_rank = (
        jnp.sum(jnp.where(same_owner, jnp.cumsum(same_owner.astype(jnp.int32), axis=0), 0), axis=1)
        - 1
    )
    own_cols = recv_buf.reshape(owners * cap, -1)[own_owner * cap + own_rank]
    neighbours = lax.all_gather(own_cols, "mp", axis=1, tiled=True)
    wq_full, wk_full, wv_full = (
        lax.all_gather(w_query, "group", axis=0, tiled=True),
        lax.all_gather(w_key, "group", axis=0, tiled=True),
        lax.all_gather(w_value, "group", axis=0, tiled=True),
    )
    query_sum = jnp.dot(full_query, wq_full, preferred_element_type=jnp.float32)
    query = query_sum.astype(jnp.bfloat16)
    wo_full = lax.all_gather(w_out, "group", axis=1, tiled=True)
    keys = jnp.dot(neighbours, wk_full, preferred_element_type=jnp.float32).astype(jnp.bfloat16)
    values = jnp.dot(neighbours, wv_full, preferred_element_type=jnp.float32).astype(jnp.bfloat16)
    key_block = keys.reshape(blocks_here, RET, heads_here, HD)
    value_block = values.reshape(blocks_here, RET, heads_here, HD)
    query_block = query.reshape(blocks_here, BLOCK, heads_here, HD)
    live = (counts > lax.axis_index("group")).astype(jnp.float32)
    scores = (
        jnp.einsum("cqhd,ckhd->chqk", query_block, key_block, preferred_element_type=jnp.float32)
        * inv_root
    )
    weights = jnp.exp(scores) * live[:, None, None, None]
    numer = jnp.einsum(
        "chqk,ckhd->cqhd",
        weights.astype(jnp.bfloat16),
        value_block,
        preferred_element_type=jnp.float32,
    )
    partial_total = jnp.sum(weights, -1)
    numer, partial_total = lax.psum((numer, partial_total), "group")
    total = partial_total + 1.0
    attn = numer / jnp.transpose(total, (0, 2, 1))[..., None]
    attn_bf = attn.reshape(rows_here, heads_here * HD).astype(jnp.bfloat16)
    out_term = jnp.dot(attn_bf, wo_full, preferred_element_type=jnp.float32)
    d_attn = contract(full_grad, wo_full).astype(jnp.bfloat16)
    d_block = d_attn.reshape(blocks_here, BLOCK, heads_here, HD)
    prob = weights / total[..., None]
    d_prob = jnp.einsum("cqhd,ckhd->chqk", d_block, value_block, preferred_element_type=jnp.float32)
    delta = jnp.sum(d_block.astype(jnp.float32) * attn, -1)
    d_score = (prob * (d_prob - jnp.transpose(delta, (0, 2, 1))[..., None])).astype(jnp.bfloat16)
    query_part = jnp.einsum(
        "chqk,ckhd->cqhd", d_score, key_block, preferred_element_type=jnp.float32
    )
    query_grad = lax.psum(query_part, "group")
    d_query = (query_grad * inv_root).astype(jnp.bfloat16).reshape(rows_here, heads_here * HD)
    d_keys = (
        jnp.einsum("chqk,cqhd->ckhd", d_score, query_block, preferred_element_type=jnp.float32)
        * inv_root
    ).astype(jnp.bfloat16)
    d_values = jnp.einsum(
        "chqk,cqhd->ckhd", prob.astype(jnp.bfloat16), d_block, preferred_element_type=jnp.float32
    ).astype(jnp.bfloat16)
    d_keys = d_keys.reshape(blocks_here * RET, heads_here * HD)
    d_values = d_values.reshape(blocks_here * RET, heads_here * HD)
    hid_term = contract(d_query, wq_full)
    out_cols, hid_cols = (
        lax.psum_scatter(
            out_term.astype(jnp.bfloat16), "mp", scatter_dimension=1, tiled=True
        ).astype(jnp.float32),
        lax.psum_scatter(
            hid_term.astype(jnp.bfloat16), "mp", scatter_dimension=1, tiled=True
        ).astype(jnp.float32),
    )
    zero_rows = jnp.zeros((tail_rows, out_cols.shape[1]), jnp.float32)
    output = jnp.concatenate([zero_rows, out_cols[:keep_rows]], 0)
    grad_hidden = jnp.concatenate([zero_rows, hid_cols[:keep_rows]], 0)
    neigh_term = contract(d_keys, wk_full) + contract(d_values, wv_full)
    neigh_cols = lax.psum_scatter(
        neigh_term.astype(jnp.bfloat16), "mp", scatter_dimension=1, tiled=True
    ).astype(jnp.float32)
    grad_neighbours = neigh_cols.reshape(blocks_here, 1, RET, neigh_cols.shape[1])
    return (output, grad_hidden, grad_neighbours)


def solution(mesh):
    return jax.shard_map(
        per_device,
        mesh=mesh,
        in_specs=(
            P("dp", "mp"),
            P("dp", "group", None),
            P("dp"),
            P(("dp", "group"), "mp"),
            P("group", "mp"),
            P("group", "mp"),
            P("group", "mp"),
            P("mp", "group"),
            P("dp", "mp"),
        ),
        out_specs=(P("dp", "mp"), P("dp", "mp"), P("dp", "group", None, "mp")),
        check_vma=False,
    )
```

profile of v0, /device:TPU:2, one launch (start us, length us, event | category | flops | bytes accessed | tf_op | source)
XLA Modules:
  0.0 972.8 jit_solution(12286093274936307989)
XLA Ops:
  12.4 40.9 %all-gather.1 = f32[16,1,256]{2,1,0:T(1,128)S(1)} all-gather(f32[1,1,256]{2,1,0:T(1,128)S(1)} %bitcast.107), channel_id=1, replica_groups=mesh['dp'=8,'mp'=16,'group'=2] {'dp','group'}, dimensions={0}, use_global_device_ids=true | all-gather | bytes 17408 | tf_op jit(solution)/shard_map/all_gather | solution.py:39
  54.8 7.9 gather_fusion
  62.7 6.0 all-to-all-start
  69.8 38.2 %all-to-all-done = bf16[16,64,512]{2,1,0:T(8,128)(2,1)S(1)} async-done(((bf16[16,64,512]{2,1,0:T(8,128)(2,1)}), bf16[16,64,512]{2,1,0:T(8,128)(2,1)S(1)}, u32[]{:S(2)}, u32[]{:S(2)}) %all-to-all-start) | async-done | bytes 1048608 | tf_op jit(solution)/shard_map/all_to_all | solution.py:50
  110.7 60.2 %all-gather.14.cloned.1.call-done = bf16[8192,256]{1,0:T(8,128)(2,1)} async-done(((bf16[4096,256]{1,0:T(8,128)(2,1)}), bf16[8192,256]{1,0:T(8,128)(2,1)}) %all-gather.14.cloned.1.call-update) | async-done | bytes 4194320 | tf_op jit(solution)/shard_map/all_gather | solution.py:60
  170.9 3.5 convolution_convert_fusion.6
  174.4 65.6 %all-gather.20.cloned.1.call-done = bf16[128,8192]{1,0:T(8,128)(2,1)} async-done(((bf16[128,512]{1,0:T(8,128)(2,1)}), bf16[128,8192]{1,0:T(8,128)(2,1)}) %all-gather.20.cloned.1.call-update) | async-done | bytes 2097168 | tf_op jit(solution)/shard_map/all_gather | solution.py:32
  240.0 113.4 %all-gather.18.cloned.1.call-done = bf16[256,8192]{1,0:T(8,128)(2,1)} async-done(((bf16[256,4096]{1,0:T(8,128)(2,1)}), bf16[256,8192]{1,0:T(8,128)(2,1)}) %all-gather.18.cloned.1.call-update) | async-done | bytes 4194320 | tf_op jit(solution)/shard_map/all_gather | solution.py:66
  353.4 4.4 convolution_convert_fusion.5
  357.8 105.4 %all-gather.10.cloned.1.call-done = bf16[8192,256]{1,0:T(8,128)(2,1)} async-done(((bf16[4096,256]{1,0:T(8,128)(2,1)}), bf16[8192,256]{1,0:T(8,128)(2,1)}) %all-gather.10.cloned.1.call-update) | async-done | bytes 4194320 | tf_op jit(solution)/shard_map/all_gather | solution.py:62
  463.2 61.3 %all-gather.22.cloned.1.call-done = bf16[256,8192]{1,0:T(8,128)(2,1)} async-done(((bf16[256,512]{1,0:T(8,128)(2,1)}), bf16[256,8192]{1,0:T(8,128)(2,1)}) %all-gather.22.cloned.1.call-update) | async-done | bytes 4194320 | tf_op jit(solution)/shard_map/all_gather | solution.py:58
  524.5 4.7 convolution_convert_fusion.4
  529.2 108.8 %all-gather.16.cloned.1.call-done = bf16[8192,256]{1,0:T(8,128)(2,1)} async-done(((bf16[4096,256]{1,0:T(8,128)(2,1)}), bf16[8192,256]{1,0:T(8,128)(2,1)}) %all-gather.16.cloned.1.call-update) | async-done | bytes 4194320 | tf_op jit(solution)/shard_map/all_gather | solution.py:61
  638.1 4.7 convolution_convert_fusion.3
  644.0 8.8 psum.22
  652.9 25.8 %all-reduce.7.cloned.1.call-done = f32[2,64,2,128]{3,1,2,0:T(8,128)} async-done(((f32[2,64,2,128]{3,1,2,0:T(8,128)}), f32[2,64,2,128]{3,1,2,0:T(8,128)}) %all-reduce.7.cloned.1.call-update) | async-done | bytes 131088 | tf_op jit(solution)/shard_map/psum | solution.py:85
  681.0 4.3 convolution_convert_fusion.1
  685.3 31.5 %all-reduce.9.cloned.1.call-done = f32[2,64,2,128]{3,1,2,0:T(8,128)} async-done(((f32[2,64,2,128]{3,1,2,0:T(8,128)}), f32[2,64,2,128]{3,1,2,0:T(8,128)}) %all-reduce.9.cloned.1.call-update) | async-done | bytes 131088 | tf_op jit(solution)/shard_map/psum | solution.py:99
  717.9 5.0 convolution_convert_fusion
  724.0 3.6 fusion.11
  727.6 3.2 fusion
  730.8 64.9 %reduce-scatter.4.cloned.1.call-done = bf16[128,512]{1,0:T(8,128)(2,1)} async-done(((bf16[128,8192]{1,0:T(8,128)(2,1)}), bf16[128,512]{1,0:T(8,128)(2,1)}) %reduce-scatter.4.cloned.1.call-update) | async-done | bytes 131088 | tf_op jit(solution)/shard_map/reduce_scatter | solution.py:112
  797.3 81.1 %reduce-scatter.6.cloned.1.call-done = bf16[128,512]{1,0:T(8,128)(2,1)} async-done(((bf16[128,8192]{1,0:T(8,128)(2,1)}), bf16[128,512]{1,0:T(8,128)(2,1)}) %reduce-scatter.6.cloned.1.call-update) | async-done | bytes 131088 | tf_op jit(solution)/shard_map/reduce_scatter | solution.py:115
  880.1 84.0 %reduce-scatter.8.cloned.1.call-done = bf16[256,512]{1,0:T(8,128)(2,1)} async-done(((bf16[256,8192]{1,0:T(8,128)(2,1)}), bf16[256,512]{1,0:T(8,128)(2,1)}) %reduce-scatter.8.cloned.1.call-update) | async-done | bytes 262160 | tf_op jit(solution)/shard_map/reduce_scatter | solution.py:123
  (86 shorter events, 20.9 us)
Async XLA Ops:
  7.2 5.2 copy-start.1
  7.2 103.5 %all-gather.12.cloned.1.call-start = ((), (), s32[]{:S(2)}) async-start(), calls=%async_computation.5 | async-start | bytes 2228224 | tf_op jit(solution)/shard_map/all_gather | solution.py:31
  8.8 162.1 %all-gather.14.cloned.1.call-start = ((), (), s32[]{:S(2)}) async-start(), calls=%async_computation.6 | async-start | bytes 6291456 | tf_op jit(solution)/shard_map/all_gather | solution.py:60
  9.6 230.4 %all-gather.20.cloned.1.call-start = ((), (), s32[]{:S(2)}) async-start(), calls=%async_computation.11 | async-start | bytes 2228224 | tf_op jit(solution)/shard_map/all_gather | solution.py:32
  11.2 342.2 %all-gather.18.cloned.1.call-start = ((), (), s32[]{:S(2)}) async-start(), calls=%async_computation.9 | async-start | bytes 6291456 | tf_op jit(solution)/shard_map/all_gather | solution.py:66
  11.8 451.4 %all-gather.10.cloned.1.call-start = ((), (), s32[]{:S(2)}) async-start(), calls=%async_computation.4 | async-start | bytes 6291456 | tf_op jit(solution)/shard_map/all_gather | solution.py:62
  62.7 47.9 %copy-start.2 = (s32[2]{0:T(128)S(1)}, s32[2]{0:T(128)}, u32[]{:S(2)}) copy-start(s32[2]{0:T(128)} %param.11) | copy-start | bytes 28
  62.7 45.2 %all-to-all-start = ((bf16[16,64,512]{2,1,0:T(8,128)(2,1)}), bf16[16,64,512]{2,1,0:T(8,128)(2,1)S(1)}, u32[]{:S(2)}, u32[]{:S(2)}) async-start(bf16[16,64,512]{2,1,0:T(8,128)(2,1)} %bitcast.4), calls=%async_computation | async-start | bytes 2097152 | tf_op jit(solution)/shard_map/all_to_all | solution.py:50
  68.7 455.8 %all-gather.22.cloned.1.call-start = ((), (), s32[]{:S(2)}) async-start(), calls=%async_computation.15 | async-start | bytes 4456448 | tf_op jit(solution)/shard_map/all_gather | solution.py:58
  109.8 528.2 %all-gather.16.cloned.1.call-start = ((), (), s32[]{:S(2)}) async-start(), calls=%async_computation.7 | async-start | bytes 6291456 | tf_op jit(solution)/shard_map/all_gather | solution.py:61
  110.6 568.1 %all-reduce.7.cloned.1.call-start = ((), (), s32[]{:S(2)}) async-start(), calls=%async_computation.8 | async-start | bytes 262144 | tf_op jit(solution)/shard_map/psum | solution.py:85
  644.0 72.9 %all-reduce.9.cloned.1.call-start = ((), (), s32[]{:S(2)}) async-start(), calls=%async_computation.12 | async-start | bytes 262144 | tf_op jit(solution)/shard_map/psum | solution.py:99
  680.9 114.8 %reduce-scatter.4.cloned.1.call-start = ((), (), s32[]{:S(2)}) async-start(), calls=%async_computation.10 | async-start | bytes 2228224 | tf_op jit(solution)/shard_map/reduce_scatter | solution.py:112
  685.3 193.2 %reduce-scatter.6.cloned.1.call-start = ((), (), s32[]{:S(2)}) async-start(), calls=%async_computation.13 | async-start | bytes 2228224 | tf_op jit(solution)/shard_map/reduce_scatter | solution.py:115
  722.9 241.2 %reduce-scatter.8.cloned.1.call-start = ((), (), s32[]{:S(2)}) async-start(), calls=%async_computation.14 | async-start | bytes 4456448 | tf_op jit(solution)/shard_map/reduce_scatter | solution.py:123
  723.9 3.6 copy-start
Sparse Core Ops, SparseCore 0:
  11.0 55.3 all-gather.11
  68.1 102.6 all-gather.13
  173.9 66.1 all-gather.19
  241.7 111.7 all-gather.17
  355.1 108.0 all-gather.9
  466.1 58.3 all-gather.21
  526.3 111.7 all-gather.15
  644.1 34.5 all-reduce.6
  681.9 34.9 all-reduce.8
  720.3 75.4 reduce-scatter.3
  799.7 78.6 reduce-scatter.5
  881.9 82.1 reduce-scatter.7
where the time goes:
time: 973 us
  waiting for transfers between devices  843 us (87%)
  blocking collectives  49.7 us (5%)
  matrix products  36.1 us (4%)
  local copies, waits for them, and re-layouts  15.7 us (2%)
  between operations  14.5 us (1%)
    all_gather x1, waiting for transfers between devices, per_device(): wo_full = lax.all_gather(w_out, 'group', axis=1, tiled=True)  113 us
    all_gather x1, waiting for transfers between devices, per_device(): lax.all_gather(w_key, 'group', axis=0, tiled=True)  109 us
    all_gather x1, waiting for transfers between devices, per_device(): lax.all_gather(w_value, 'group', axis=0, tiled=True)  105 us
    reduce_scatter x1, waiting for transfers between devices, per_device(): lax.psum_scatter(neigh_term.astype(jnp.bfloat16), 'mp', scatter_dimension...  84 us
    reduce_scatter x1, waiting for transfers between devices, per_device(): lax.psum_scatter(hid_term.astype(jnp.bfloat16), 'mp', scatter_dimension=1...  81.1 us
    all_gather x1, waiting for transfers between devices, per_device(): lax.all_gather(grad_rows, 'mp', axis=1, tiled=True)  65.6 us
    reduce_scatter x1, waiting for transfers between devices, per_device(): lax.psum_scatter(out_term.astype(jnp.bfloat16), 'mp', scatter_dimension=1...  64.9 us
    all_gather x1, waiting for transfers between devices, per_device(): neighbours = lax.all_gather(own_cols, 'mp', axis=1, tiled=True)  61.3 us
  transfers between devices with their start and end apart: 13, of which 12 were waited for; matrix products, arithmetic and copies ran while one was open for 5% of the time, Pallas kernels for 0%

commit v1 on v0

--- a/solution.py
+++ b/solution.py
@@ -7,6 +7,15 @@
 HD = 128
 BLOCK = 64
 RET = 128
+replace_axis_part = lambda patch: jnp.concatenate(
+    lax.all_to_all(
+        jnp.stack([patch for _ in range(lax.axis_size("group"))], axis=0),
+        "group",
+        split_axis=0,
+        concat_axis=0,
+    ),
+    1,
+)
 
 
 def contract(left, right):
@@ -63,7 +72,7 @@
     )
     query_sum = jnp.dot(full_query, wq_full, preferred_element_type=jnp.float32)
     query = query_sum.astype(jnp.bfloat16)
-    wo_full = lax.all_gather(w_out, "group", axis=1, tiled=True)
+    wo_full = replace_axis_part(w_out)
     keys = jnp.dot(neighbours, wk_full, preferred_element_type=jnp.float32).astype(jnp.bfloat16)
     values = jnp.dot(neighbours, wv_full, preferred_element_type=jnp.float32).astype(jnp.bfloat16)
     key_block = keys.reshape(blocks_here, RET, heads_here, HD)

time: 973 us -> 940 us (0.966)
  waiting for transfers between devices: 843 us -> 799 us
    all_gather x1 -> x0, waiting for transfers between devices: 113 us -> none  [per_device(): wo_full = lax.all_gather(w_out, 'group', axis=1, tiled=True)]
    all_gather x1, waiting for transfers between devices: 65.6 us -> 123 us  [per_device(): lax.all_gather(grad_rows, 'mp', axis=1, tiled=True)]
    all_gather x1, waiting for transfers between devices: 60.2 us -> 70.2 us  [per_device(): lax.all_gather(w_query, 'group', axis=0, tiled=True)]
  transfers between devices with their start and end apart: 13 -> 13, of which waited for: 12 -> 11; matrix products, arithmetic and copies ran while one was open for 5% -> 6% of each run, Pallas kernels for 0% -> 0%
where the time goes in v1:
time: 940 us
  waiting for transfers between devices  799 us (85%)
  blocking collectives  49.7 us (5%)
  matrix products  36.1 us (4%)
  local copies, waits for them, and re-layouts  18.9 us (2%)
  between operations  14.2 us (2%)
  starting transfers between devices  12.4 us (1%)
  other arithmetic  9.53 us (1%)
    all_gather x1, waiting for transfers between devices, per_device(): lax.all_gather(grad_rows, 'mp', axis=1, tiled=True)  123 us
    all_gather x1, waiting for transfers between devices, per_device(): lax.all_gather(w_value, 'group', axis=0, tiled=True)  110 us
    all_gather x1, waiting for transfers between devices, per_device(): lax.all_gather(w_key, 'group', axis=0, tiled=True)  109 us
    reduce_scatter x1, waiting for transfers between devices, per_device(): lax.psum_scatter(neigh_term.astype(jnp.bfloat16), 'mp', scatter_dimension...  84.2 us
    reduce_scatter x1, waiting for transfers between devices, per_device(): lax.psum_scatter(hid_term.astype(jnp.bfloat16), 'mp', scatter_dimension=1...  81 us
    all_gather x1, waiting for transfers between devices, per_device(): lax.all_gather(w_query, 'group', axis=0, tiled=True)  70.2 us
    reduce_scatter x1, waiting for transfers between devices, per_device(): lax.psum_scatter(out_term.astype(jnp.bfloat16), 'mp', scatter_dimension=1...  65 us
    all_gather x1, waiting for transfers between devices, per_device(): neighbours = lax.all_gather(own_cols, 'mp', axis=1, tiled=True)  61.3 us
  transfers between devices with their start and end apart: 13, of which 11 were waited for; matrix products, arithmetic and copies ran while one was open for 6% of the time, Pallas kernels for 0%

profile of v1, /device:TPU:2, one launch (start us, length us, event | category | flops | bytes accessed | tf_op | source)
XLA Modules:
  0.0 939.7 jit_solution(14721480694538555153)
XLA Ops:
  11.8 40.9 %all-gather.1 = f32[16,1,256]{2,1,0:T(1,128)S(1)} all-gather(f32[1,1,256]{2,1,0:T(1,128)S(1)} %bitcast.112), channel_id=1, replica_groups=mesh['dp'=8,'mp'=16,'group'=2] {'dp','group'}, dimensions={0}, use_global_device_ids=true | all-gather | bytes 17408 | tf_op jit(solution)/shard_map/all_gather | solution.py:48
  54.2 7.8 gather_fusion
  62.1 6.0 all-to-all-start
  69.1 37.6 %all-to-all-done = bf16[16,64,512]{2,1,0:T(8,128)(2,1)S(1)} async-done(((bf16[16,64,512]{2,1,0:T(8,128)(2,1)}), bf16[16,64,512]{2,1,0:T(8,128)(2,1)S(1)}, u32[]{:S(2)}, u32[]{:S(2)}) %all-to-all-start) | async-done | bytes 1048608 | tf_op jit(solution)/shard_map/all_to_all | solution.py:59
  108.6 3.3 copy.62
  114.2 5.9 all-to-all-start.1
  120.7 70.2 %all-gather.13.cloned.1.call-done = bf16[8192,256]{1,0:T(8,128)(2,1)} async-done(((bf16[4096,256]{1,0:T(8,128)(2,1)}), bf16[8192,256]{1,0:T(8,128)(2,1)}) %all-gather.13.cloned.1.call-update) | async-done | bytes 4194320 | tf_op jit(solution)/shard_map/all_gather | solution.py:69
  190.9 3.5 convolution_convert_fusion.6
  194.5 122.6 %all-gather.17.cloned.1.call-done = bf16[128,8192]{1,0:T(8,128)(2,1)} async-done(((bf16[128,512]{1,0:T(8,128)(2,1)}), bf16[128,8192]{1,0:T(8,128)(2,1)}) %all-gather.17.cloned.1.call-update) | async-done | bytes 2097168 | tf_op jit(solution)/shard_map/all_gather | solution.py:41
  317.1 3.5 convolution_convert_fusion.5
  320.7 109.9 %all-gather.9.cloned.1.call-done = bf16[8192,256]{1,0:T(8,128)(2,1)} async-done(((bf16[4096,256]{1,0:T(8,128)(2,1)}), bf16[8192,256]{1,0:T(8,128)(2,1)}) %all-gather.9.cloned.1.call-update) | async-done | bytes 4194320 | tf_op jit(solution)/shard_map/all_gather | solution.py:71
  430.6 61.3 %all-gather.19.cloned.1.call-done = bf16[256,8192]{1,0:T(8,128)(2,1)} async-done(((bf16[256,512]{1,0:T(8,128)(2,1)}), bf16[256,8192]{1,0:T(8,128)(2,1)}) %all-gather.19.cloned.1.call-update) | async-done | bytes 4194320 | tf_op jit(solution)/shard_map/all_gather | solution.py:67
  491.8 4.7 convolution_convert_fusion.4
  496.6 108.7 %all-gather.15.cloned.1.call-done = bf16[8192,256]{1,0:T(8,128)(2,1)} async-done(((bf16[4096,256]{1,0:T(8,128)(2,1)}), bf16[8192,256]{1,0:T(8,128)(2,1)}) %all-gather.15.cloned.1.call-update) | async-done | bytes 4194320 | tf_op jit(solution)/shard_map/all_gather | solution.py:70
  605.2 4.7 convolution_convert_fusion.3
  611.2 8.8 psum.22
  620.0 25.8 %all-reduce.7.cloned.1.call-done = f32[2,64,2,128]{3,1,2,0:T(8,128)} async-done(((f32[2,64,2,128]{3,1,2,0:T(8,128)}), f32[2,64,2,128]{3,1,2,0:T(8,128)}) %all-reduce.7.cloned.1.call-update) | async-done | bytes 131088 | tf_op jit(solution)/shard_map/psum | solution.py:94
  648.2 5.0 convolution_convert_fusion.1
  653.3 30.7 %all-reduce.9.cloned.1.call-done = f32[2,64,2,128]{3,1,2,0:T(8,128)} async-done(((f32[2,64,2,128]{3,1,2,0:T(8,128)}), f32[2,64,2,128]{3,1,2,0:T(8,128)}) %all-reduce.9.cloned.1.call-update) | async-done | bytes 131088 | tf_op jit(solution)/shard_map/psum | solution.py:108
  685.0 5.0 convolution_convert_fusion
  691.1 3.6 fusion.11
  698.0 65.0 %reduce-scatter.4.cloned.1.call-done = bf16[128,512]{1,0:T(8,128)(2,1)} async-done(((bf16[128,8192]{1,0:T(8,128)(2,1)}), bf16[128,512]{1,0:T(8,128)(2,1)}) %reduce-scatter.4.cloned.1.call-update) | async-done | bytes 131088 | tf_op jit(solution)/shard_map/reduce_scatter | solution.py:121
  764.7 81.0 %reduce-scatter.6.cloned.1.call-done = bf16[128,512]{1,0:T(8,128)(2,1)} async-done(((bf16[128,8192]{1,0:T(8,128)(2,1)}), bf16[128,512]{1,0:T(8,128)(2,1)}) %reduce-scatter.6.cloned.1.call-update) | async-done | bytes 131088 | tf_op jit(solution)/shard_map/reduce_scatter | solution.py:124
  847.2 84.2 %reduce-scatter.8.cloned.1.call-done = bf16[256,512]{1,0:T(8,128)(2,1)} async-done(((bf16[256,8192]{1,0:T(8,128)(2,1)}), bf16[256,512]{1,0:T(8,128)(2,1)}) %reduce-scatter.8.cloned.1.call-update) | async-done | bytes 262160 | tf_op jit(solution)/shard_map/reduce_scatter | solution.py:132
  (87 shorter events, 25.7 us)
Async XLA Ops:
  7.2 4.6 copy-start.1
  7.2 113.6 %all-gather.11.cloned.1.call-start = ((), (), s32[]{:S(2)}) async-start(), calls=%async_computation.6 | async-start | bytes 2228224 | tf_op jit(solution)/shard_map/all_gather | solution.py:40
  8.8 182.1 %all-gather.13.cloned.1.call-start = ((), (), s32[]{:S(2)}) async-start(), calls=%async_computation.7 | async-start | bytes 6291456 | tf_op jit(solution)/shard_map/all_gather | solution.py:69
  9.6 307.6 %all-gather.17.cloned.1.call-start = ((), (), s32[]{:S(2)}) async-start(), calls=%async_computation.11 | async-start | bytes 2228224 | tf_op jit(solution)/shard_map/all_gather | solution.py:41
  11.2 419.3 %all-gather.9.cloned.1.call-start = ((), (), s32[]{:S(2)}) async-start(), calls=%async_computation.5 | async-start | bytes 6291456 | tf_op jit(solution)/shard_map/all_gather | solution.py:71
  62.1 44.6 %all-to-all-start = ((bf16[16,64,512]{2,1,0:T(8,128)(2,1)}), bf16[16,64,512]{2,1,0:T(8,128)(2,1)S(1)}, u32[]{:S(2)}, u32[]{:S(2)}) async-start(bf16[16,64,512]{2,1,0:T(8,128)(2,1)} %bitcast.4), calls=%async_computation | async-start | bytes 2097152 | tf_op jit(solution)/shard_map/all_to_all | solution.py:59
  68.1 423.7 %all-gather.19.cloned.1.call-start = ((), (), s32[]{:S(2)}) async-start(), calls=%async_computation.15 | async-start | bytes 4456448 | tf_op jit(solution)/shard_map/all_gather | solution.py:67
  114.2 6.5 copy-start.2
  114.2 202.9 %all-to-all-start.1 = ((bf16[2,256,4096]{1,2,0:T(8,128)(2,1)}), bf16[2,256,4096]{1,2,0:T(8,128)(2,1)}, u32[]{:S(2)}, u32[]{:S(2)}) async-start(bf16[2,256,4096]{1,2,0:T(8,128)(2,1)} %pad_maximum_fusion), calls=%async_computation.1 | async-start | bytes 8388608 | tf_op jit(solution)/shard_map/all_to_all | solution.py:11
  120.1 485.1 %all-gather.15.cloned.1.call-start = ((), (), s32[]{:S(2)}) async-start(), calls=%async_computation.8 | async-start | bytes 6291456 | tf_op jit(solution)/shard_map/all_gather | solution.py:70
  120.6 525.2 %all-reduce.7.cloned.1.call-start = ((), (), s32[]{:S(2)}) async-start(), calls=%async_computation.9 | async-start | bytes 262144 | tf_op jit(solution)/shard_map/psum | solution.py:94
  611.1 72.9 %all-reduce.9.cloned.1.call-start = ((), (), s32[]{:S(2)}) async-start(), calls=%async_computation.12 | async-start | bytes 262144 | tf_op jit(solution)/shard_map/psum | solution.py:108
  648.1 114.9 %reduce-scatter.4.cloned.1.call-start = ((), (), s32[]{:S(2)}) async-start(), calls=%async_computation.10 | async-start | bytes 2228224 | tf_op jit(solution)/shard_map/reduce_scatter | solution.py:121
  653.2 192.4 %reduce-scatter.6.cloned.1.call-start = ((), (), s32[]{:S(2)}) async-start(), calls=%async_computation.13 | async-start | bytes 2228224 | tf_op jit(solution)/shard_map/reduce_scatter | solution.py:124
  690.1 241.3 %reduce-scatter.8.cloned.1.call-start = ((), (), s32[]{:S(2)}) async-start(), calls=%async_computation.14 | async-start | bytes 4456448 | tf_op jit(solution)/shard_map/reduce_scatter | solution.py:132
  691.1 3.6 copy-start
Sparse Core Ops, SparseCore 0:
  11.0 55.3 all-gather.10
  68.1 122.7 all-gather.12
  193.9 123.1 all-gather.16
  318.8 111.7 all-gather.8
  433.4 58.3 all-gather.18
  493.5 111.7 all-gather.14
  611.3 34.5 all-reduce.6
  649.0 34.9 all-reduce.8
  687.6 75.4 reduce-scatter.3
  766.9 78.6 reduce-scatter.5
  849.3 82.0 reduce-scatter.7
